TPU v7x, 32 devices: a whole 2x2x4 slice. The times are simulated.
32 devices in a mesh: groups: 2 (over x), right: 4 (over y, core), left: 4 (over z).
Axes of the slice: x: 2, y: 2, z: 4, core: 2. Of those that a mesh axis runs over, the one named last changes fastest.
Arguments:
- left_act: bfloat16 [4096, 8192], P(('groups', 'right'), 'left'), parts along dimension 0, may hold values from -15 to 15
- right_act: bfloat16 [4096, 4096], P(('groups', 'left'), 'right'), parts along dimension 0, may hold values from -15 to 15
- counts: int32 [512, 128], P(('groups', 'left'), 'right'), parts along dimension 0, may hold values from 512 to 2048
- w_out: bfloat16 [1024, 128], replicated, may hold values from -0.1875 to 0.1875
Outputs:
- pair_update: float32 [512, 128, 128], P(('groups', 'left'), 'right'), parts along dimension 0
There are 2 independent parts, one for each index of `groups`. A program takes and returns all parts, laid end to end along the dimension named above; an argument that names none is the same for every part. Nothing has to cross between parts.
All inputs are finite; a program needn't handle non-finite values.
Results may differ from a plain program's by a relative error of at most 0.0029.
Values may be sent and summed in bfloat16 or wider, within the bound.
A program may use at most 128 MiB of HBM per device.

v0:
```python
import jax
import jax.numpy as jnp
from jax import lax
from jax.sharding import PartitionSpec as P

CH = 32


def contract_rows(first, second):
    return lax.dot_general(
        first, second, (((0,), (0,)), ((), ())), preferred_element_type=jnp.float32
    )


def shards(left_act, right_act, counts, w_out):
    left_dev = counts.shape[0]
    right_dev = counts.shape[1]
    left_full = lax.all_gather(left_act, "right", axis=0, tiled=True)
    outer = contract_rows(left_full, lax.all_gather(right_act, "left", axis=0, tiled=True))
    flat = (
        outer.reshape(left_dev, CH, right_dev, CH)
        .transpose(0, 2, 1, 3)
        .reshape(left_dev * right_dev, CH * CH)
    )
    flat = flat.astype(jnp.bfloat16)
    projected = jnp.dot(flat, w_out, preferred_element_type=jnp.float32).reshape(
        left_dev, right_dev, w_out.shape[1]
    )
    return projected / counts.astype(jnp.float32)[:, :, None]


def solution(mesh):
    in_specs = (
        P(("groups", "right"), "left"),
        P(("groups", "left"), "right"),
        P(("groups", "left"), "right"),
        P(),
    )
    out_specs = P(("groups", "left"), "right", None)
    return jax.shard_map(shards, mesh=mesh, in_specs=in_specs, out_specs=out_specs, check_vma=False)
```

profile of v0, /device:TPU:0, one launch (start us, length us, event | category | flops | bytes accessed | tf_op | source)
XLA Modules:
  0.0 220.9 jit_solution(8785365857728057451)
XLA Ops:
  6.5 0.0 copy-start
  6.5 0.0 all-gather.5.cloned.1.call-start
  6.5 0.7 all-gather.5.cloned.1.call-update
  7.3 0.0 all-gather.3.cloned.1.call-start
  7.3 0.7 all-gather.3.cloned.1.call-update
  8.0 0.7 convert_element_type.20
  8.7 0.1 copy.9
  8.8 83.6 %all-gather.5.cloned.1.call-done = bf16[2048,1024]{1,0:T(8,128)(2,1)} async-done(((bf16[512,1024]{1,0:T(8,128)(2,1)}), bf16[2048,1024]{1,0:T(8,128)(2,1)}) %all-gather.5.cloned.1.call-update) | async-done | bytes 4194320 | tf_op jit(solution)/shard_map/all_gather | solution.py:19
  92.4 58.3 %all-gather.3.cloned.1.call-done = bf16[2048,2048]{1,0:T(8,128)(2,1)} async-done(((bf16[512,2048]{1,0:T(8,128)(2,1)}), bf16[2048,2048]{1,0:T(8,128)(2,1)}) %all-gather.3.cloned.1.call-update) | async-done | bytes 8388624 | tf_op jit(solution)/shard_map/all_gather | solution.py:18
  150.7 14.0 %convolution_convert_fusion = bf16[2048,1024]{1,0:T(8,128)(2,1)} fusion(bf16[2048,2048]{1,0:T(8,128)(2,1)} %all-gather.3.cloned.1.call-done, bf16[2048,1024]{1,0:T(8,128)(2,1)} %all-gather.5.cloned.1.call-done), kind=kOutput, calls=%fused_computation | convolution fusion | flops 8592031744 | bytes 16777216 | tf_op jit(solution)/shard_map/dot_general | solution.py:10
  164.7 20.3 %convert_element_type.17 = bf16[64,32,32,32]{3,2,1,0:T(8,128)(2,1)} reshape(bf16[2048,1024]{1,0:T(8,128)(2,1)} %convolution_convert_fusion) | data formatting | bytes 8388608 | tf_op jit(solution)/shard_map/convert_element_type | solution.py:25
  185.0 21.7 %copy.7 = bf16[64,32,32,32]{0,3,2,1:T(8,128)(2,1)} copy(bf16[64,32,32,32]{3,1,2,0:T(8,128)(2,1)} %bitcast.8) | data formatting | bytes 8388608 | tf_op jit(solution)/shard_map/convert_element_type | solution.py:25
  206.7 0.0 copy-done
  206.7 5.7 %fusion = f32[64,32,128]{2,0,1:T(8,128)S(1)} fusion(bf16[64,32,1024]{0,2,1:T(8,128)(2,1)} %bitcast.9, bf16[1024,128]{1,0:T(8,128)(2,1)S(1)} %copy-done), kind=kOutput, calls=%fused_computation.2 | convolution fusion | flops 536870912 | bytes 5505024 | tf_op jit(solution)/shard_map/dot_general | solution.py:26
  212.5 1.7 copy_divide_fusion
Async XLA Ops:
  6.5 200.2 %copy-start = (bf16[1024,128]{1,0:T(8,128)(2,1)S(1)}, bf16[1024,128]{1,0:T(8,128)(2,1)}, u32[]{:S(2)}) copy-start(bf16[1024,128]{1,0:T(8,128)(2,1)} %param.7) | copy-start | bytes 786436
  6.5 85.9 %all-gather.5.cloned.1.call-start = ((), (), s32[]{:S(2)}) async-start(), calls=%async_computation.1 | async-start | bytes 5242880 | tf_op jit(solution)/shard_map/all_gather | solution.py:19
  7.3 143.5 %all-gather.3.cloned.1.call-start = ((), (), s32[]{:S(2)}) async-start(), calls=%async_computation | async-start | bytes 10485760 | tf_op jit(solution)/shard_map/all_gather | solution.py:18
Sparse Core Ops, SparseCore 0:
  8.9 83.4 all-gather.4
  94.0 56.7 all-gather.2
where the time goes:
time: 222 us; the launch traced here: 221 us
  waiting for transfers between devices  143 us (64%)
  local copies, waits for them, and re-layouts  42.1 us (19%)
  matrix products  19.7 us (9%)
  between operations  13.4 us (6%)
  other arithmetic  2.38 us (1%)
    all_gather x1, waiting for transfers between devices, shards(): lax.all_gather(right_act, 'left', axis=0, tiled=True)  83.6 us
    all_gather x1, waiting for transfers between devices, shards(): left_full = lax.all_gather(left_act, 'right', axis=0, tiled=True)  58.3 us
    convert_element_type x2, local copies, waits for them, and re-layouts, shards(): flat = flat.astype(jnp.bfloat16)  42 us
    dot_general x1, matrix products, contract_rows(): lax.dot_general(first, second, (((0,), (0,)), ((), ())), preferred_elemen...  14 us
    dot_general x1, matrix products, shards(): jnp.dot(flat, w_out, preferred_element_type=jnp.float32)  5.75 us
  transfers between devices with their start and end apart: 2, of which 2 were waited for; matrix products, arithmetic and copies ran while one was open for 0% of the time, Pallas kernels for 0%

commit v1 on v0

v1 whole, which is shorter than its diff:
```python
import functools

import jax
import jax.numpy as jnp
from jax import lax
from jax.experimental import pallas as pl
from jax.experimental.pallas import tpu as pltpu
from jax.sharding import PartitionSpec as P

CH = 32
CORES = 2
MESH = pl.DeviceIdType.MESH


def lane_quads(tiles):
    lane = lax.broadcasted_iota(jnp.int32, tiles[0].shape, 1)
    low = lane < 64
    even = (lane % 64) < 32
    stage = [None] * 4
    for c in range(2):
        a, b = tiles[c], tiles[c + 2]
        stage[c] = jnp.where(low, a, pltpu.roll(b, 64, 1))
        stage[c + 2] = jnp.where(low, pltpu.roll(a, 64, 1), b)
    outs = [None] * 4
    for half in range(2):
        a, b = stage[2 * half], stage[2 * half + 1]
        outs[2 * half] = jnp.where(even, a, pltpu.roll(b, 32, 1))
        outs[2 * half + 1] = jnp.where(even, pltpu.roll(a, 96, 1), b)
    return outs


def kernel(sizes, left_ref, right_ref, w_ref, out_ref, left_full, right_full, left_t, acc, flat,
           z_send, z_recv, y_send, y_recv, s_send, s_recv, own_sem):
    n_z, n_r, q_z, q_y = sizes
    n_y = n_r // CORES
    rows_l, width_l = left_ref.shape
    rows_r, width_r = right_ref.shape
    piece_r = width_r // q_z
    piece_l = rows_l // q_y
    left_dev = width_l // CH
    right_dev = width_r // CH
    seqs = left_t.shape[1]
    z = lax.axis_index("left")
    r = lax.axis_index("right")
    y = r // CORES
    k = r % CORES

    def z_dev(pos):
        return {"left": pos}

    def y_dev(pos):
        return {"right": pos * CORES + k}

    sib_dev = {"right": y * CORES + (1 - k)}

    barrier = pltpu.get_barrier_semaphore()

    def greet(dev):
        pl.semaphore_signal(barrier, inc=1, device_id=dev, device_id_type=MESH)

    greet(sib_dev)
    for pos, n, dev in ((z, n_z, z_dev), (y, n_y, y_dev)):
        pl.when(pos + 1 < n)(functools.partial(greet, dev(pos + 1)))
        pl.when(pos >= 1)(functools.partial(greet, dev(pos - 1)))
    total = 1 + (z + 1 < n_z).astype(jnp.int32) + (z >= 1).astype(jnp.int32)
    total = total + (y + 1 < n_y).astype(jnp.int32) + (y >= 1).astype(jnp.int32)
    pl.semaphore_wait(barrier, total)

    def z_slot(chunk, q):
        return right_full.at[pl.ds(pl.multiple_of(chunk * rows_r, rows_r), rows_r), pl.ds(q * piece_r, piece_r)]

    def z_copy(side, step, q):
        sign = 1 - 2 * side
        chunk = z - sign * step
        src = right_ref.at[:, pl.ds(q * piece_r, piece_r)] if step == 0 else z_slot(chunk, q)
        at = step * q_z + q
        return pltpu.make_async_remote_copy(
            src_ref=src, dst_ref=z_slot(chunk, q), send_sem=z_send.at[side, at], recv_sem=z_recv.at[side, at],
            device_id=z_dev(z + sign), device_id_type=MESH)

    def z_sends(side, step):
        near = z + 1 < n_z if side == 0 else z >= 1
        far = z - step >= 0 if side == 0 else z + step < n_z
        return jnp.logical_and(near, far)

    def z_arrives(side, step):
        return z - step - 1 >= 0 if side == 0 else z + step + 1 < n_z

    def z_wait(side, step, q):
        sign = 1 - 2 * side
        slot = z_slot(z - sign * (step + 1), q)
        pltpu.make_async_copy(slot, slot, z_recv.at[side, step * q_z + q]).wait()

    def l_slot(chunk, q):
        return left_full.at[pl.ds(pl.multiple_of(chunk * rows_l + q * piece_l, piece_l), piece_l), :]

    def l_own(q):
        return left_ref.at[pl.ds(q * piece_l, piece_l), :]

    def y_copy(side, step, q):
        sign = 1 - 2 * side
        chunk = (y - sign * step) * CORES + k
        at = step * q_y + q
        return pltpu.make_async_remote_copy(
            src_ref=l_own(q) if step == 0 else l_slot(chunk, q), dst_ref=l_slot(chunk, q),
            send_sem=y_send.at[side, at], recv_sem=y_recv.at[side, at],
            device_id=y_dev(y + sign), device_id_type=MESH)

    def y_sends(side, step):
        near = y + 1 < n_y if side == 0 else y >= 1
        far = y - step >= 0 if side == 0 else y + step < n_y
        return jnp.logical_and(near, far)

    def y_arrives(side, step):
        return y - step - 1 >= 0 if side == 0 else y + step + 1 < n_y

    def y_wait(side, step, q):
        sign = 1 - 2 * side
        slot = l_slot((y - sign * (step + 1)) * CORES + k, q)
        pltpu.make_async_copy(slot, slot, y_recv.at[side, step * q_y + q]).wait()

    def s_at(side, step, q):
        if step < 0:
            return q
        return (1 + side * (n_y - 1) + step) * q_y + q

    def s_copy(side, step, q):
        sign = 1 - 2 * side
        chunk = (y - sign * (step + 1)) * CORES + k if step >= 0 else r
        at = s_at(side, step, q)
        return pltpu.make_async_remote_copy(
            src_ref=l_own(q) if step < 0 else l_slot(chunk, q), dst_ref=l_slot(chunk, q),
            send_sem=s_send.at[at], recv_sem=s_recv.at[at],
            device_id=sib_dev, device_id_type=MESH)

    def s_wait(side, step, q):
        sign = 1 - 2 * side
        y_from = y - sign * (step + 1) if step >= 0 else y
        slot = l_slot(y_from * CORES + (1 - k), q)
        pltpu.make_async_copy(slot, slot, s_recv.at[s_at(side, step, q)]).wait()

    tile = 256

    def turn(src, first_row, chunk, q):
        col = pl.multiple_of(chunk * rows_l + q * piece_l, piece_l)

        def body(m, carry):
            at = pl.multiple_of(m * tile, tile)
            left_t[pl.ds(at, tile), pl.ds(col, piece_l)] = src[pl.ds(first_row, piece_l), pl.ds(at, tile)].T
            return carry

        lax.fori_loop(0, width_l // tile, body, 0)

    def turn_full(chunk, q):
        turn(left_full, pl.multiple_of(chunk * rows_l + q * piece_l, piece_l), chunk, q)

    own = pltpu.make_async_copy(right_ref, right_full.at[pl.ds(pl.multiple_of(z * rows_r, rows_r), rows_r), :], own_sem)
    own.start()
    for q in range(max(q_z, q_y)):
        for side in range(2):
            if q < q_z:
                pl.when(z_sends(side, 0))(lambda side=side, q=q: z_copy(side, 0, q).start())
            if q < q_y:
                pl.when(y_sends(side, 0))(lambda side=side, q=q: y_copy(side, 0, q).start())
    for q in range(q_y):
        s_copy(0, -1, q).start()
    for q in range(q_y):
        turn(left_ref, q * piece_l, r, q)
    for q in range(q_y):
        s_wait(0, -1, q)
        turn_full(y * CORES + (1 - k), q)

    def z_tick(step, q):
        for side in range(2):
            @pl.when(z_arrives(side, step))
            def _():
                z_wait(side, step, q)
                if step + 1 < n_z - 1:
                    pl.when(z_sends(side, step + 1))(lambda: z_copy(side, step + 1, q).start())

    def y_tick(step, q):
        for side in range(2):
            @pl.when(y_arrives(side, step))
            def _():
                y_wait(side, step, q)
                s_copy(side, step, q).start()
                if step + 1 < n_y - 1:
                    pl.when(y_sends(side, step + 1))(lambda: y_copy(side, step + 1, q).start())

        for side in range(2):
            @pl.when(y_arrives(side, step))
            def _():
                sign = 1 - 2 * side
                y_from = y - sign * (step + 1)
                turn_full(y_from * CORES + k, q)
                s_wait(side, step, q)
                turn_full(y_from * CORES + (1 - k), q)

    y_ticks = [(step, q) for step in range(n_y - 1) for q in range(q_y)]
    for t in range((n_z - 2) * q_z):
        z_tick(t // q_z, t % q_z)
        if t % 2 == 1 and y_ticks:
            y_tick(*y_ticks.pop(0))
    for tick in y_ticks:
        y_tick(*tick)
    own.wait()

    block = 512
    at_end = jnp.logical_or(z == 0, z == n_z - 1)
    base = jnp.where(z == 0, 0, rows_r)
    base = pl.multiple_of(base, rows_r)

    def product(q, first, depth, add):
        cols = pl.ds(q * piece_r, piece_r)

        def body(m, carry):
            rows = pl.ds(pl.multiple_of(m * block, block), block)
            value = jnp.dot(left_t[rows, pl.ds(first, depth)], right_full[pl.ds(first, depth), cols],
                            preferred_element_type=jnp.float32)
            for part in range(piece_r // 128):
                some = value[:, part * 128:(part + 1) * 128]
                slab = q * (piece_r // 128) + part
                acc[slab, rows, :] = acc[slab, rows, :] + some if add else some
            return carry

        lax.fori_loop(0, width_l // block, body, 0)

    def first_part(q):
        @pl.when(at_end)
        def _():
            product(q, base, seqs - rows_r, False)

        @pl.when(jnp.logical_not(at_end))
        def _():
            product(q, 0, seqs, False)

    for q in range(q_z):
        first_part(q)

    def finish(q):
        heads = piece_r // CH
        for quad in range(heads // 4):
            slab = acc.at[q * (piece_r // 128) + quad]
            for cq in range(CH // 4):
                tiles = [slab[pl.ds(cq * 4 + c, left_dev, stride=CH), :] for c in range(4)]
                for j, value in enumerate(lane_quads(tiles)):
                    flat[pl.ds((quad * 4 + j) * left_dev, left_dev), pl.ds(cq * 128, 128)] = value.astype(jnp.bfloat16)
        projected = jnp.dot(flat[...], w_ref[...], preferred_element_type=jnp.float32)
        for j in range(heads):
            out_ref[pl.ds(q * heads + j, left_dev, stride=right_dev), :] = projected[j * left_dev:(j + 1) * left_dev, :]

    last = n_z - 2
    for q in range(q_z):
        z_tick(last, q)

        @pl.when(at_end)
        def _():
            far = jnp.where(z == 0, (n_z - 1) * rows_r, 0)
            product(q, pl.multiple_of(far, rows_r), rows_r, True)

        finish(q)

    for side in range(2):
        for step in range(n_z - 1):
            for q in range(q_z):
                pl.when(z_sends(side, step))(lambda side=side, step=step, q=q: z_copy(side, step, q).wait_send())
        for step in range(n_y - 1):
            for q in range(q_y):
                pl.when(y_sends(side, step))(lambda side=side, step=step, q=q: y_copy(side, step, q).wait_send())
                pl.when(y_arrives(side, step))(lambda side=side, step=step, q=q: s_copy(side, step, q).wait_send())
    for q in range(q_y):
        s_copy(0, -1, q).wait_send()


def solution(mesh):
    n_z, n_r = mesh.shape["left"], mesh.shape["right"]
    n_y = n_r // CORES

    def shards(left_act, right_act, counts, w_out):
        rows_l, width_l = left_act.shape
        rows_r, width_r = right_act.shape
        seqs = rows_r * n_z
        left_dev, right_dev = counts.shape
        pair = w_out.shape[1]
        q_z = width_r // 256
        q_y = rows_l // max(128, rows_l // 4)
        projected = pl.pallas_call(
            functools.partial(kernel, (n_z, n_r, q_z, q_y)),
            out_shape=jax.ShapeDtypeStruct((left_dev * right_dev, pair), jnp.float32),
            in_specs=[pl.BlockSpec(memory_space=pltpu.VMEM)] * 3,
            out_specs=pl.BlockSpec(memory_space=pltpu.VMEM),
            scratch_shapes=[
                pltpu.VMEM((seqs, width_l), jnp.bfloat16),
                pltpu.VMEM((seqs, width_r), jnp.bfloat16),
                pltpu.VMEM((width_l, seqs), jnp.bfloat16),
                pltpu.VMEM((width_r // 128, width_l, 128), jnp.float32),
                pltpu.VMEM((width_r // q_z // CH * left_dev, CH * CH), jnp.bfloat16),
                pltpu.SemaphoreType.DMA((2, (n_z - 1) * q_z)),
                pltpu.SemaphoreType.DMA((2, (n_z - 1) * q_z)),
                pltpu.SemaphoreType.DMA((2, (n_y - 1) * q_y)),
                pltpu.SemaphoreType.DMA((2, (n_y - 1) * q_y)),
                pltpu.SemaphoreType.DMA(((2 * n_y - 1) * q_y,)),
                pltpu.SemaphoreType.DMA(((2 * n_y - 1) * q_y,)),
                pltpu.SemaphoreType.DMA,
            ],
            compiler_params=pltpu.CompilerParams(
                collective_id=0, has_side_effects=True, vmem_limit_bytes=56 * 1024 * 1024
            ),
            name="pair_mean",
        )(left_act, right_act, w_out)
        projected = projected.reshape(left_dev, right_dev, pair)
        return projected / counts.astype(jnp.float32)[:, :, None]

    in_specs = (
        P(("groups", "right"), "left"),
        P(("groups", "left"), "right"),
        P(("groups", "left"), "right"),
        P(),
    )
    out_specs = P(("groups", "left"), "right", None)
    return jax.shard_map(shards, mesh=mesh, in_specs=in_specs, out_specs=out_specs, check_vma=False)
```

time: 222 us -> 83.4 us (0.38)
  waiting for transfers between devices: 143 us -> 0 us
  Pallas kernels: 0 us -> 79.7 us
  local copies, waits for them, and re-layouts: 42.1 us -> 0.08 us
  matrix products: 19.7 us -> 0 us
  between operations: 13.4 us -> 0.01 us
    all_gather x2 -> x0, waiting for transfers between devices: 142 us -> none  [the longest x1 83.6 us: shards(): lax.all_gather(right_act, 'left', axis=0, tiled=True)]
    pallas_call x0 -> x1, Pallas kernels: none -> 79.7 us  [shards(): pl.pallas_call(functools.partial(kernel, (n_z, n_r, q_z, q_y)), out_shape...]
    convert_element_type x2 -> x0, local copies, waits for them, and re-layouts: 42 us -> none  [shards(): flat = flat.astype(jnp.bfloat16)]
    dot_general x2 -> x0, matrix products: 19.7 us -> none  [the longest x1 14 us: contract_rows(): lax.dot_general(first, second, (((0,), (0,)), ((), ())), preferred_elemen...]
  transfers between devices with their start and end apart: 2 -> 0, of which waited for: 2 -> 0; matrix products, arithmetic and copies ran while one was open for 0% -> 0% of each run, Pallas kernels for 0% -> 0%
where the time goes in v1:
time: 83.4 us; the launch traced here: 83 us
  Pallas kernels  79.7 us (96%)
  other arithmetic  3.26 us (4%)
    pallas_call x1, Pallas kernels, shards(): pl.pallas_call(functools.partial(kernel, (n_z, n_r, q_z, q_y)), out_shape...  79.7 us
    div x1, other arithmetic, shards(): return projected / counts.astype(jnp.float32)[:, :, None]  2.54 us

profile of v1, /device:TPU:0, one launch (start us, length us, event | category | flops | bytes accessed | tf_op | source)
XLA Modules:
  0.0 83.0 jit_solution(8610875360918089473)
XLA Ops:
  0.0 0.7 convert_element_type.3
  0.7 0.1 copy.5
  0.8 79.7 %pair_mean.1 = f32[2048,128]{1,0:T(8,128)} custom-call(bf16[512,2048]{1,0:T(8,128)(2,1)} %left_ref.1, bf16[512,1024]{1,0:T(8,128)(2,1)} %right_ref.1, bf16[1024,128]{1,0:T(8,128)(2,1)} %w_ref.1), custom_call_target="tpu_custom_call" | custom-call | tf_op jit(solution)/shard_map/pair_mean/pallas_call | solution.py:287
  80.5 2.5 %broadcast_divide_fusion = f32[64,32,128]{2,1,0:T(8,128)} fusion(f32[64,32,128]{2,1,0:T(8,128)} %bitcast.1, f32[64,32]{1,0:T(8,128)S(1)} %copy.5), kind=kLoop, calls=%fused_computation | loop fusion | flops 262144 | bytes 2105344 | tf_op jit(solution)/shard_map/div | solution.py:312

commit v2 on v1

--- a/solution.py
+++ b/solution.py
@@ -30,8 +30,11 @@
 
 
 def kernel(sizes, left_ref, right_ref, w_ref, out_ref, left_full, right_full, left_t, acc, flat,
-           z_send, z_recv, y_send, y_recv, s_send, s_recv, own_sem):
+           z_send, z_recv, y_send, y_recv, s_send, s_recv, own_sem, *extra):
     n_z, n_r, q_z, q_y = sizes
+    lends = len(extra) > 0
+    if lends:
+        lent, lent_t, part_out, part_in, ready, l_send, l_recv, ls_send, ls_recv, p_send, p_recv = extra
     n_y = n_r // CORES
     rows_l, width_l = left_ref.shape
     rows_r, width_r = right_ref.shape
@@ -51,6 +54,14 @@
     def y_dev(pos):
         return {"right": pos * CORES + k}
 
+    at_end = jnp.logical_or(z == 0, z == n_z - 1)
+    at_helper = jnp.logical_not(at_end)
+    moved = y + 1
+    lender = jnp.where(z == 1, 0, n_z - 1)
+    helper = jnp.where(z == 0, 1, n_z - 2)
+    owner = r == moved
+    half = jnp.where(owner, 1, 0)
+
     sib_dev = {"right": y * CORES + (1 - k)}
 
     barrier = pltpu.get_barrier_semaphore()
@@ -81,10 +92,20 @@
     def z_sends(side, step):
         near = z + 1 < n_z if side == 0 else z >= 1
         far = z - step >= 0 if side == 0 else z + step < n_z
-        return jnp.logical_and(near, far)
+        go = jnp.logical_and(near, far)
+        if lends:
+            sign = 1 - 2 * side
+            kept = jnp.logical_and(z + sign == (n_z - 1 if side == 0 else 0), z - sign * step == moved)
+            go = jnp.logical_and(go, jnp.logical_not(kept))
+        return go
 
     def z_arrives(side, step):
-        return z - step - 1 >= 0 if side == 0 else z + step + 1 < n_z
+        comes = z - step - 1 >= 0 if side == 0 else z + step + 1 < n_z
+        if lends:
+            sign = 1 - 2 * side
+            kept = jnp.logical_and(at_end, z - sign * (step + 1) == moved)
+            comes = jnp.logical_and(comes, jnp.logical_not(kept))
+        return comes
 
     def z_wait(side, step, q):
         sign = 1 - 2 * side
@@ -156,23 +177,75 @@
 
     own = pltpu.make_async_copy(right_ref, right_full.at[pl.ds(pl.multiple_of(z * rows_r, rows_r), rows_r), :], own_sem)
     own.start()
-    for q in range(max(q_z, q_y)):
-        for side in range(2):
-            if q < q_z:
+    def z_start():
+        for q in range(q_z):
+            for side in range(2):
                 pl.when(z_sends(side, 0))(lambda side=side, q=q: z_copy(side, 0, q).start())
-            if q < q_y:
-                pl.when(y_sends(side, 0))(lambda side=side, q=q: y_copy(side, 0, q).start())
+
+    def lent_rows(part, p):
+        return pl.ds(pl.multiple_of(part * (rows_l // 2) + p * piece_l, piece_l), piece_l)
+
+    def lend(p, from_own):
+        base_row = pl.multiple_of(moved * rows_l + half * (rows_l // 2) + p * piece_l, piece_l)
+        return pltpu.make_async_remote_copy(
+            src_ref=left_ref.at[lent_rows(half, p), :] if from_own else left_full.at[pl.ds(base_row, piece_l), :],
+            dst_ref=lent.at[lent_rows(half, p), :], send_sem=l_send.at[p], recv_sem=l_recv.at[p],
+            device_id=z_dev(helper), device_id_type=MESH)
+
+    def lent_across(p):
+        slot = lent.at[lent_rows(half, p), :]
+        return pltpu.make_async_remote_copy(
+            src_ref=slot, dst_ref=slot, send_sem=ls_send.at[p], recv_sem=ls_recv.at[p],
+            device_id=sib_dev, device_id_type=MESH)
+
+    def part_copy(q):
+        return pltpu.make_async_remote_copy(
+            src_ref=part_out.at[q], dst_ref=part_in.at[q], send_sem=p_send.at[q], recv_sem=p_recv.at[q],
+            device_id=z_dev(lender), device_id_type=MESH)
+
+    lent_pieces = q_y // 2
+    end_owner = jnp.logical_and(at_end, owner)
+    end_other = jnp.logical_and(at_end, jnp.logical_not(owner))
+
     for q in range(q_y):
         s_copy(0, -1, q).start()
     for q in range(q_y):
+        for side in range(2):
+            pl.when(y_sends(side, 0))(lambda side=side, q=q: y_copy(side, 0, q).start())
+    if lends:
+        pl.when(at_helper)(z_start)
+
+        @pl.when(end_owner)
+        def _():
+            for p in range(lent_pieces):
+                lend(p, True).start()
+            z_start()
+
+        for p in range(lent_pieces):
+            s_wait(0, -1, p)
+
+        @pl.when(end_other)
+        def _():
+            for p in range(lent_pieces):
+                lend(p, False).start()
+            z_start()
+    else:
+        z_start()
+    for q in range(q_y):
         turn(left_ref, q * piece_l, r, q)
     for q in range(q_y):
-        s_wait(0, -1, q)
+        if not lends or q >= lent_pieces:
+            s_wait(0, -1, q)
         turn_full(y * CORES + (1 - k), q)
 
-    def z_tick(step, q):
+    def z_tick(step, q, only=None):
         for side in range(2):
-            @pl.when(z_arrives(side, step))
+            arrives = z_arrives(side, step)
+            if only is not None:
+                from_end = z == (1 if side == 0 else n_z - 2)
+                arrives = jnp.logical_and(arrives, from_end if only else jnp.logical_not(from_end))
+
+            @pl.when(arrives)
             def _():
                 z_wait(side, step, q)
                 if step + 1 < n_z - 1:
@@ -196,27 +269,20 @@
                 s_wait(side, step, q)
                 turn_full(y_from * CORES + (1 - k), q)
 
-    y_ticks = [(step, q) for step in range(n_y - 1) for q in range(q_y)]
-    for t in range((n_z - 2) * q_z):
-        z_tick(t // q_z, t % q_z)
-        if t % 2 == 1 and y_ticks:
-            y_tick(*y_ticks.pop(0))
-    for tick in y_ticks:
-        y_tick(*tick)
-    own.wait()
-
     block = 512
-    at_end = jnp.logical_or(z == 0, z == n_z - 1)
     base = jnp.where(z == 0, 0, rows_r)
     base = pl.multiple_of(base, rows_r)
 
-    def product(q, first, depth, add):
+    def product(q, terms, add):
         cols = pl.ds(q * piece_r, piece_r)
 
         def body(m, carry):
             rows = pl.ds(pl.multiple_of(m * block, block), block)
-            value = jnp.dot(left_t[rows, pl.ds(first, depth)], right_full[pl.ds(first, depth), cols],
-                            preferred_element_type=jnp.float32)
+            value = None
+            for turned, col, first, depth in terms:
+                one = jnp.dot(turned[rows, pl.ds(col, depth)], right_full[pl.ds(first, depth), cols],
+                              preferred_element_type=jnp.float32)
+                value = one if value is None else value + one
             for part in range(piece_r // 128):
                 some = value[:, part * 128:(part + 1) * 128]
                 slab = q * (piece_r // 128) + part
@@ -225,40 +291,123 @@
 
         lax.fori_loop(0, width_l // block, body, 0)
 
-    def first_part(q):
-        @pl.when(at_end)
-        def _():
-            product(q, base, seqs - rows_r, False)
-
-        @pl.when(jnp.logical_not(at_end))
-        def _():
-            product(q, 0, seqs, False)
-
-    for q in range(q_z):
-        first_part(q)
-
-    def finish(q):
-        heads = piece_r // CH
+    def chunk_term(chunk):
+        first = pl.multiple_of(chunk * rows_r, rows_r)
+        return (left_t, first, first, rows_r)
+
+    heads = piece_r // CH
+
+    def project(q):
         for quad in range(heads // 4):
             slab = acc.at[q * (piece_r // 128) + quad]
             for cq in range(CH // 4):
                 tiles = [slab[pl.ds(cq * 4 + c, left_dev, stride=CH), :] for c in range(4)]
                 for j, value in enumerate(lane_quads(tiles)):
                     flat[pl.ds((quad * 4 + j) * left_dev, left_dev), pl.ds(cq * 128, 128)] = value.astype(jnp.bfloat16)
-        projected = jnp.dot(flat[...], w_ref[...], preferred_element_type=jnp.float32)
+        return jnp.dot(flat[...], w_ref[...], preferred_element_type=jnp.float32)
+
+    def put(q, projected):
         for j in range(heads):
             out_ref[pl.ds(q * heads + j, left_dev, stride=right_dev), :] = projected[j * left_dev:(j + 1) * left_dev, :]
 
-    last = n_z - 2
-    for q in range(q_z):
-        z_tick(last, q)
+    y_ticks = [(step, q) for step in range(n_y - 1) for q in range(q_y)]
+    if lends:
+        def take_lent(p):
+            slot = lent.at[lent_rows(half, p), :]
+            pltpu.make_async_copy(slot, slot, l_recv.at[p]).wait()
+            lent_across(p).start()
+
+        def turn_lent(part, p):
+            def body(m, carry):
+                at = pl.multiple_of(m * tile, tile)
+                lent_t[pl.ds(at, tile), lent_rows(part, p)] = lent[lent_rows(part, p), pl.ds(at, tile)].T
+                return carry
+
+            lax.fori_loop(0, width_l // tile, body, 0)
+
+        def use_lent(p):
+            turn_lent(half, p)
+            slot = lent.at[lent_rows(1 - half, p), :]
+            pltpu.make_async_copy(slot, slot, ls_recv.at[p]).wait()
+            turn_lent(1 - half, p)
+
+        for q in range(q_z):
+            z_tick(0, q, only=False)
+            if q % 2 == 1:
+                y_tick(*y_ticks.pop(0))
+                pl.when(at_helper)(functools.partial(take_lent, q // 2))
+                pl.when(at_helper)(functools.partial(use_lent, q // 2))
+        own.wait()
+        for q in range(q_z):
+            z_tick(0, q, only=True)
+            z_tick(1, q)
+
+            @pl.when(at_helper)
+            def _():
+                product(q, [(lent_t, 0, pl.multiple_of(moved * rows_r, rows_r), rows_r)], False)
+                part_out[q] = project(q).astype(jnp.bfloat16)
+
+            if q % 2 == 1:
+                y_tick(*y_ticks.pop(0))
+
+        @pl.when(at_helper)
+        def _():
+            for q in range(q_z):
+                part_copy(q).start()
+
+        for q in range(q_z):
+            @pl.when(at_end)
+            def _():
+                product(q, [chunk_term(z), chunk_term(n_z - 1 - moved)], False)
+
+            @pl.when(at_helper)
+            def _():
+                product(q, [(left_t, 0, 0, seqs)], False)
+                put(q, project(q))
 
         @pl.when(at_end)
         def _():
-            far = jnp.where(z == 0, (n_z - 1) * rows_r, 0)
-            product(q, pl.multiple_of(far, rows_r), rows_r, True)
-
-        finish(q)
+            for q in range(q_z):
+                z_tick(2, q)
+                product(q, [chunk_term(n_z - 1 - z)], True)
+                ready[q] = project(q)
+            for q in range(q_z):
+                slot = part_in.at[q]
+                pltpu.make_async_copy(slot, slot, p_recv.at[q]).wait()
+                put(q, ready[q] + part_in[q].astype(jnp.float32))
+            for p in range(lent_pieces):
+                lend(p, True).wait_send()
+
+        @pl.when(at_helper)
+        def _():
+            for p in range(lent_pieces):
+                lent_across(p).wait_send()
+            for q in range(q_z):
+                part_copy(q).wait_send()
+    else:
+        for t in range((n_z - 2) * q_z):
+            z_tick(t // q_z, t % q_z)
+            if t % 2 == 1 and y_ticks:
+                y_tick(*y_ticks.pop(0))
+        for tick in y_ticks:
+            y_tick(*tick)
+        own.wait()
+        for q in range(q_z):
+            @pl.when(at_end)
+            def _():
+                product(q, [(left_t, base, base, seqs - rows_r)], False)
+
+            @pl.when(at_helper)
+            def _():
+                product(q, [(left_t, 0, 0, seqs)], False)
+        for q in range(q_z):
+            z_tick(n_z - 2, q)
+
+            @pl.when(at_end)
+            def _():
+                product(q, [chunk_term(jnp.where(z == 0, n_z - 1, 0))], True)
+
+            put(q, project(q))
 
     for side in range(2):
         for step in range(n_z - 1):
@@ -284,6 +433,16 @@
         pair = w_out.shape[1]
         q_z = width_r // 256
         q_y = rows_l // max(128, rows_l // 4)
+        lends = n_z == 4 and n_y == 2 and rows_l == rows_r and q_z == 4 and q_y == 4
+        extra = [
+            pltpu.VMEM((rows_l, width_l), jnp.bfloat16),
+            pltpu.VMEM((width_l, rows_l), jnp.bfloat16),
+            pltpu.VMEM((q_z, left_dev * right_dev // q_z, pair), jnp.bfloat16),
+            pltpu.VMEM((q_z, left_dev * right_dev // q_z, pair), jnp.bfloat16),
+            pltpu.VMEM((q_z, left_dev * right_dev // q_z, pair), jnp.float32),
+            *[pltpu.SemaphoreType.DMA((2,))] * 4,
+            *[pltpu.SemaphoreType.DMA((q_z,))] * 2,
+        ]
         projected = pl.pallas_call(
             functools.partial(kernel, (n_z, n_r, q_z, q_y)),
             out_shape=jax.ShapeDtypeStruct((left_dev * right_dev, pair), jnp.float32),
@@ -302,6 +461,7 @@
                 pltpu.SemaphoreType.DMA(((2 * n_y - 1) * q_y,)),
                 pltpu.SemaphoreType.DMA(((2 * n_y - 1) * q_y,)),
                 pltpu.SemaphoreType.DMA,
+                *(extra if lends else []),
             ],
             compiler_params=pltpu.CompilerParams(
                 collective_id=0, has_side_effects=True, vmem_limit_bytes=56 * 1024 * 1024

time: 83.4 us -> 105 us (1.26)
  the two profiles are of different devices: /device:TPU:0 before, /device:TPU:19 now
where the time goes in v2:
time: 105 us
  Pallas kernels  102 us (97%)
  other arithmetic  3.26 us (3%)
    pallas_call x1, Pallas kernels, shards(): pl.pallas_call(functools.partial(kernel, (n_z, n_r, q_z, q_y)), out_shape...  102 us
    div x1, other arithmetic, shards(): return projected / counts.astype(jnp.float32)[:, :, None]  2.54 us

profile of v2, /device:TPU:19, one launch (start us, length us, event | category | flops | bytes accessed | tf_op | source)
XLA Modules:
  0.0 105.0 jit_solution(16165446177983667762)
XLA Ops:
  0.0 0.7 convert_element_type.3
  0.7 0.1 copy.5
  0.8 101.7 %pair_mean.1 = f32[2048,128]{1,0:T(8,128)} custom-call(bf16[512,2048]{1,0:T(8,128)(2,1)} %left_ref.1, bf16[512,1024]{1,0:T(8,128)(2,1)} %right_ref.1, bf16[1024,128]{1,0:T(8,128)(2,1)} %w_ref.1), custom_call_target="tpu_custom_call" | custom-call | tf_op jit(solution)/shard_map/pair_mean/pallas_call | solution.py:446
  102.5 2.5 %broadcast_divide_fusion = f32[64,32,128]{2,1,0:T(8,128)} fusion(f32[64,32,128]{2,1,0:T(8,128)} %bitcast.1, f32[64,32]{1,0:T(8,128)S(1)} %copy.5), kind=kLoop, calls=%fused_computation | loop fusion | flops 262144 | bytes 2105344 | tf_op jit(solution)/shard_map/div | solution.py:472

commit v3 on v1

--- a/solution.py
+++ b/solution.py
@@ -29,8 +29,8 @@
     return outs
 
 
-def kernel(sizes, left_ref, right_ref, w_ref, out_ref, left_full, right_full, left_t, acc, flat,
-           z_send, z_recv, y_send, y_recv, s_send, s_recv, own_sem):
+def kernel(sizes, left_ref, right_ref, counts_ref, w_hbm, out_ref, w_ref, counts_in, cover, out_v, left_full, right_full, left_t, acc, flat,
+           z_send, z_recv, y_send, y_recv, s_send, s_recv, own_sem, out_sem):
     n_z, n_r, q_z, q_y = sizes
     n_y = n_r // CORES
     rows_l, width_l = left_ref.shape
@@ -154,18 +154,27 @@
     def turn_full(chunk, q):
         turn(left_full, pl.multiple_of(chunk * rows_l + q * piece_l, piece_l), chunk, q)
 
-    own = pltpu.make_async_copy(right_ref, right_full.at[pl.ds(pl.multiple_of(z * rows_r, rows_r), rows_r), :], own_sem)
-    own.start()
     for q in range(max(q_z, q_y)):
         for side in range(2):
             if q < q_z:
                 pl.when(z_sends(side, 0))(lambda side=side, q=q: z_copy(side, 0, q).start())
             if q < q_y:
                 pl.when(y_sends(side, 0))(lambda side=side, q=q: y_copy(side, 0, q).start())
+    own_left = pltpu.make_async_copy(left_ref, left_full.at[pl.ds(pl.multiple_of(r * rows_l, rows_l), rows_l), :], own_sem.at[0])
+    own = pltpu.make_async_copy(right_ref, right_full.at[pl.ds(pl.multiple_of(z * rows_r, rows_r), rows_r), :], own_sem.at[1])
+    weights = pltpu.make_async_copy(w_hbm, w_ref, own_sem.at[2])
+    counts_copy = pltpu.make_async_copy(counts_ref, counts_in, own_sem.at[3])
+    for copy in (own_left, own, weights, counts_copy):
+        copy.start()
     for q in range(q_y):
         s_copy(0, -1, q).start()
+    own_left.wait()
     for q in range(q_y):
-        turn(left_ref, q * piece_l, r, q)
+        turn_full(r, q)
+    counts_copy.wait()
+    counted = counts_in[...].astype(jnp.float32)
+    for j in range(right_dev):
+        cover[j] = jnp.broadcast_to(counted[:, j:j + 1], (left_dev, cover.shape[2]))
     for q in range(q_y):
         s_wait(0, -1, q)
         turn_full(y * CORES + (1 - k), q)
@@ -204,6 +213,7 @@
     for tick in y_ticks:
         y_tick(*tick)
     own.wait()
+    weights.wait()
 
     block = 512
     at_end = jnp.logical_or(z == 0, z == n_z - 1)
@@ -242,13 +252,19 @@
         for quad in range(heads // 4):
             slab = acc.at[q * (piece_r // 128) + quad]
             for cq in range(CH // 4):
-                tiles = [slab[pl.ds(cq * 4 + c, left_dev, stride=CH), :] for c in range(4)]
+                tiles = [slab[pl.ds(cq * 4 + c, left_dev, stride=CH), :].astype(jnp.bfloat16) for c in range(4)]
                 for j, value in enumerate(lane_quads(tiles)):
-                    flat[pl.ds((quad * 4 + j) * left_dev, left_dev), pl.ds(cq * 128, 128)] = value.astype(jnp.bfloat16)
+                    flat[pl.ds((quad * 4 + j) * left_dev, left_dev), pl.ds(cq * 128, 128)] = value
         projected = jnp.dot(flat[...], w_ref[...], preferred_element_type=jnp.float32)
         for j in range(heads):
-            out_ref[pl.ds(q * heads + j, left_dev, stride=right_dev), :] = projected[j * left_dev:(j + 1) * left_dev, :]
-
+            value = projected[j * left_dev:(j + 1) * left_dev, :] / cover[q * heads + j]
+            out_v.at[q].reshape(left_dev * heads, value.shape[1])[pl.ds(j, left_dev, stride=heads), :] = value
+        out_copy(q).start()
+
+    def out_copy(q):
+        return pltpu.make_async_copy(out_v.at[q], out_ref.at[:, pl.ds(q * heads_q, heads_q), :], out_sem.at[q])
+
+    heads_q = piece_r // CH
     last = n_z - 2
     for q in range(q_z):
         z_tick(last, q)
@@ -270,6 +286,8 @@
                 pl.when(y_arrives(side, step))(lambda side=side, step=step, q=q: s_copy(side, step, q).wait_send())
     for q in range(q_y):
         s_copy(0, -1, q).wait_send()
+    for q in range(q_z):
+        out_copy(q).wait()
 
 
 def solution(mesh):
@@ -286,10 +304,14 @@
         q_y = rows_l // max(128, rows_l // 4)
         projected = pl.pallas_call(
             functools.partial(kernel, (n_z, n_r, q_z, q_y)),
-            out_shape=jax.ShapeDtypeStruct((left_dev * right_dev, pair), jnp.float32),
-            in_specs=[pl.BlockSpec(memory_space=pltpu.VMEM)] * 3,
-            out_specs=pl.BlockSpec(memory_space=pltpu.VMEM),
+            out_shape=jax.ShapeDtypeStruct((left_dev, right_dev, pair), jnp.float32),
+            in_specs=[pl.BlockSpec(memory_space=pl.ANY)] * 4,
+            out_specs=pl.BlockSpec(memory_space=pl.ANY),
             scratch_shapes=[
+                pltpu.VMEM(w_out.shape, w_out.dtype),
+                pltpu.VMEM(counts.shape, counts.dtype),
+                pltpu.VMEM((right_dev, left_dev, pair), jnp.float32),
+                pltpu.VMEM((q_z, left_dev, right_dev // q_z, pair), jnp.float32),
                 pltpu.VMEM((seqs, width_l), jnp.bfloat16),
                 pltpu.VMEM((seqs, width_r), jnp.bfloat16),
                 pltpu.VMEM((width_l, seqs), jnp.bfloat16),
@@ -301,15 +323,15 @@
                 pltpu.SemaphoreType.DMA((2, (n_y - 1) * q_y)),
                 pltpu.SemaphoreType.DMA(((2 * n_y - 1) * q_y,)),
                 pltpu.SemaphoreType.DMA(((2 * n_y - 1) * q_y,)),
-                pltpu.SemaphoreType.DMA,
+                pltpu.SemaphoreType.DMA((4,)),
+                pltpu.SemaphoreType.DMA((q_z,)),
             ],
             compiler_params=pltpu.CompilerParams(
                 collective_id=0, has_side_effects=True, vmem_limit_bytes=56 * 1024 * 1024
             ),
             name="pair_mean",
-        )(left_act, right_act, w_out)
-        projected = projected.reshape(left_dev, right_dev, pair)
-        return projected / counts.astype(jnp.float32)[:, :, None]
+        )(left_act, right_act, counts, w_out)
+        return projected
 
     in_specs = (
         P(("groups", "right"), "left"),

time: 83.4 us -> 81 us (0.971)
  local copies, waits for them, and re-layouts: 0.08 us -> 3.68 us
  other arithmetic: 3.26 us -> 0 us
  Pallas kernels: 79.7 us -> 77.1 us
    unnamed x0 -> x2, local copies, waits for them, and re-layouts: none -> 3.68 us
    div x1 -> x0, other arithmetic: 2.54 us -> none  [shards(): return projected / counts.astype(jnp.float32)[:, :, None]]
    pallas_call x1, Pallas kernels: 79.7 us -> 77.1 us  [shards(): pl.pallas_call(functools.partial(kernel, (n_z, n_r, q_z, q_y)), out_shape...]
where the time goes in v3:
time: 81 us; the launch traced here: 80.8 us
  Pallas kernels  77.1 us (95%)
  local copies, waits for them, and re-layouts  3.68 us (5%)
    pallas_call x1, Pallas kernels, shards(): pl.pallas_call(functools.partial(kernel, (n_z, n_r, q_z, q_y)), out_shape...  77.1 us
    unnamed x2, local copies, waits for them, and re-layouts  3.68 us

profile of v3, /device:TPU:0, one launch (start us, length us, event | category | flops | bytes accessed | tf_op | source)
XLA Modules:
  0.0 80.8 jit_solution(12981823083975440347)
XLA Ops:
  0.0 1.4 %copy.5.counts_ref = s32[64,32]{1,0:T(8,128)} copy(s32[64,32]{0,1:T(8,128)} %param.6) | data formatting | bytes 16384 | tf_op args[2]
  1.4 77.1 %pair_mean.1 = f32[64,32,128]{2,1,0:T(8,128)} custom-call(bf16[512,2048]{1,0:T(8,128)(2,1)} %left_ref.1, bf16[512,1024]{1,0:T(8,128)(2,1)} %right_ref.1, s32[64,32]{1,0:T(8,128)} %copy.5.counts_ref, bf16[1024,128]{1,0:T(8,128)(2,1)} %w_hbm.1), custom_call_target="tpu_custom_call" | custom-call | tf_op jit(solution)/shard_map/pair_mean/pallas_call | solution.py:305
  78.6 2.3 %copy.7 = f32[64,32,128]{2,1,0:T(8,128)} copy(f32[64,32,128]{2,1,0:T(8,128)} %pair_mean.1) | data formatting | bytes 2097152

commit v4 on v3

--- a/solution.py
+++ b/solution.py
@@ -215,7 +215,7 @@
     own.wait()
     weights.wait()
 
-    block = 512
+    block = 1024
     at_end = jnp.logical_or(z == 0, z == n_z - 1)
     base = jnp.where(z == 0, 0, rows_r)
     base = pl.multiple_of(base, rows_r)

time: 81 us -> 80.7 us (level)
  no operation moved by 1% of the time
where the time goes in v4:
time: 80.7 us; the launch traced here: 80.5 us
  Pallas kernels  76.8 us (95%)
  local copies, waits for them, and re-layouts  3.68 us (5%)
    pallas_call x1, Pallas kernels, shards(): pl.pallas_call(functools.partial(kernel, (n_z, n_r, q_z, q_y)), out_shape...  76.8 us
    unnamed x2, local copies, waits for them, and re-layouts  3.68 us

profile of v4, /device:TPU:0, one launch (start us, length us, event | category | flops | bytes accessed | tf_op | source)
XLA Modules:
  0.0 80.5 jit_solution(15863092043330643589)
XLA Ops:
  0.0 1.4 %copy.5.counts_ref = s32[64,32]{1,0:T(8,128)} copy(s32[64,32]{0,1:T(8,128)} %param.6) | data formatting | bytes 16384 | tf_op args[2]
  1.4 76.8 %pair_mean.1 = f32[64,32,128]{2,1,0:T(8,128)} custom-call(bf16[512,2048]{1,0:T(8,128)(2,1)} %left_ref.1, bf16[512,1024]{1,0:T(8,128)(2,1)} %right_ref.1, s32[64,32]{1,0:T(8,128)} %copy.5.counts_ref, bf16[1024,128]{1,0:T(8,128)(2,1)} %w_hbm.1), custom_call_target="tpu_custom_call" | custom-call | tf_op jit(solution)/shard_map/pair_mean/pallas_call | solution.py:305
  78.2 2.3 %copy.7 = f32[64,32,128]{2,1,0:T(8,128)} copy(f32[64,32,128]{2,1,0:T(8,128)} %pair_mean.1) | data formatting | bytes 2097152
